TPU v7x, 32 devices: a whole 2x2x4 slice. The times are simulated.
32 devices in a mesh: lines: 4 (over y, x), buses: 8 (over z, core).
Axes of the slice: x: 2, y: 2, z: 4, core: 2. Of those that a mesh axis runs over, the one named last changes fastest.
Arguments:
- ptdf: bfloat16 [4096, 10240], P('lines', 'buses'), may hold values from -0.078125 to 0.078125
- load: float32 [384, 10240], P(None, 'buses'), may hold values from 0.03 to 3.8, as said below
- ratings: float32 [32768], replicated, may hold values from 0.3 to 3
- line_index: int32 [4096], P('lines'), may hold values from 0 to 32767
- gen_bus: int32 [2048], P('buses'), may hold values from 0 to 10239, as said below
- gen_quad: float32 [2048], P('buses'), may hold values from 0.05 to 0.5
- gen_lin: float32 [2048], P('buses'), may hold values from 0.5 to 2.5
- gen_max: float32 [2048], P('buses'), may hold values from 0.8 to 4
- gen_start: float32 [384, 2048], P(None, 'buses'), may hold values from 0 to 2
- stor_bus: int32 [1024], P('buses'), may hold values from 0 to 1279
- stor_quad: float32 [1024], P('buses'), may hold values from 0.05 to 0.5
- stor_rate: float32 [1024], P('buses'), may hold values from 0.3 to 1.5
- stor_energy: float32 [1024], P('buses'), may hold values from 1 to 8
- stor_start: float32 [384, 1024], P(None, 'buses'), may hold values from -0.5 to 0.5
- lam_start: float32 [384], replicated, may hold values from -4 to 4
- mu_start: float32 [384, 4096], P(None, ('lines', 'buses')), may hold values from -3 to 3
- omega_start: float32 [384, 1024], P(None, 'buses'), may hold values from -2 to 2
Outputs:
- gen_out: float32 [384, 2048], P(None, 'buses')
- stor_out: float32 [384, 1024], P(None, 'buses')
- lam_out: float32 [384], replicated
- mu_out: float32 [384, 4096], P(None, ('lines', 'buses'))
- omega_out: float32 [384, 1024], P(None, 'buses')
Inputs may be any that keep to these rules, and one draw needn't show every extreme that they name: `gen_bus`: of the 256 generators of one area at most 32 sit on the buses of any one area (1280 consecutive buses); in every draw one area holds exactly 32 generators of every area, and the others of an area spread over the remaining areas as evenly as counts allow. `load`: loads are positive.
All inputs are finite; a program needn't handle non-finite values.
Results may differ from a plain program's by a relative error of at most 0.0075.
Values may be sent and summed in bfloat16 or wider, within the bound.
A program may use at most 64 MiB of HBM per device.

v0:
```python
import jax
import jax.numpy as jnp
from jax import lax
from jax.sharding import PartitionSpec as P

HOURS = 24


TAU = 0.25
SIGMA_FLOW = 4.0
SIGMA_STORE = 0.25
KAPPA = 1.0
THETA = 0.5


def reverse_cum(values, hour_count):
    total_rows, columns = values.shape
    shaped = values.reshape(total_rows // hour_count, hour_count, columns)
    summed = jnp.flip(jnp.cumsum(jnp.flip(shaped, 1), axis=1), 1)
    return summed.reshape(total_rows, columns)


def forward_cum(values, hour_count):
    total_rows, columns = values.shape
    shaped = values.reshape(total_rows // hour_count, hour_count, columns)
    return jnp.cumsum(shaped, axis=1).reshape(total_rows, columns)


def dual_step(dual_now, image_term, step_size, low_bound, high_bound):
    shifted = dual_now + step_size * image_term
    return shifted - step_size * jnp.clip(shifted / step_size, low_bound, high_bound)


def shards(
    ptdf,
    load,
    ratings,
    line_index,
    gen_bus,
    gen_quad,
    gen_lin,
    gen_max,
    gen_start,
    stor_bus,
    stor_quad,
    stor_rate,
    stor_energy,
    stor_start,
    lam_start,
    mu_start,
    omega_start,
):
    row_count = load.shape[0]
    line_count, bus_count = ptdf.shape
    gen_count = gen_bus.shape[0]
    stor_count = stor_bus.shape[0]
    device_count = lax.axis_size("buses")
    slot_count = max(8, (gen_count + device_count - 1) // device_count)
    slot_width = device_count * slot_count
    share_len = line_count // device_count
    share_start = lax.axis_index("buses") * share_len
    target = gen_bus // bus_count
    local_bus = gen_bus % bus_count
    target_hit = (target[:, None] == jnp.arange(device_count, dtype=jnp.int32)[None, :]).astype(
        jnp.int32
    )
    rank_in = jnp.sum(target_hit * jnp.cumsum(target_hit, axis=0), axis=1) - 1
    column = target * slot_count + rank_in
    slot_ids = jnp.full((slot_width,), -1, jnp.int32).at[column].set(local_bus)
    arrived = lax.all_to_all(slot_ids[None, :], "buses", split_axis=1, concat_axis=1, tiled=True)
    arrived_bus = jnp.maximum(arrived[0], 0)
    limit_block = jnp.take(ratings, line_index)
    limit_share = lax.dynamic_slice_in_dim(limit_block, share_start, share_len)
    hour_of = jnp.arange(row_count, dtype=jnp.int32) % HOURS
    last_hour = (hour_of == HOURS - 1)[:, None]
    half_energy = (0.5 * stor_energy)[None, :]
    low_bound = jnp.where(last_hour, jnp.zeros_like(half_energy), -half_energy)
    high_bound = jnp.where(last_hour, jnp.zeros_like(half_energy), half_energy)
    load_total = jnp.sum(load, axis=1)
    total_units = (gen_count + stor_count) * device_count
    dual_flow = mu_start
    gen_now, stor_now = (gen_start, stor_start)
    gen_old, stor_old = (gen_start, stor_start)
    price_level, dual_store = (lam_start, omega_start)
    for iteration in range(2):
        if iteration == 0:
            gen_mid, stor_mid = (gen_now, stor_now)
        else:
            gen_mid = gen_now + THETA * (gen_now - gen_old)
            stor_mid = stor_now + THETA * (stor_now - stor_old)
        dual_low = lax.all_gather(dual_flow.astype(jnp.bfloat16), "buses", axis=1, tiled=True)
        partial_value = jnp.dot(dual_low, ptdf, preferred_element_type=jnp.float32)
        bus_price = lax.psum(partial_value.astype(jnp.bfloat16), "lines").astype(jnp.float32)
        gen_part = jnp.take(
            lax.all_to_all(
                jnp.take(bus_price, arrived_bus, axis=1).astype(jnp.bfloat16),
                "buses",
                split_axis=1,
                concat_axis=1,
                tiled=True,
            ).astype(jnp.float32),
            column,
            axis=1,
        )
        stor_price = jnp.take(bus_price, stor_bus, axis=1)
        gen_grad = 2.0 * gen_quad * gen_mid + gen_lin + price_level[:, None] + gen_part
        gen_next = jnp.clip(gen_mid - TAU * gen_grad, 0.0, gen_max)
        stor_grad = (
            2.0 * stor_quad * stor_mid
            + price_level[:, None]
            + stor_price
            + reverse_cum(dual_store, HOURS)
        )
        stor_next = jnp.clip(stor_mid - TAU * stor_grad, -stor_rate, stor_rate)
        gen_bar = 2.0 * gen_next - gen_now
        stor_bar = 2.0 * stor_next - stor_now
        balance_term = jnp.sum(gen_bar, axis=1) + jnp.sum(stor_bar, axis=1) - load_total
        stor_inject = jnp.zeros((row_count, bus_count), jnp.float32).at[:, stor_bus].add(stor_bar)
        slotted = jnp.zeros((gen_bar.shape[0], slot_width), jnp.float32).at[:, column].set(gen_bar)
        received = lax.all_to_all(
            slotted.astype(jnp.bfloat16), "buses", split_axis=1, concat_axis=1, tiled=True
        ).astype(slotted.dtype)
        empty = jnp.zeros((received.shape[0], bus_count), jnp.float32)
        injection = empty.at[:, arrived_bus].add(received) + stor_inject - load
        inj_low = injection.astype(jnp.bfloat16)
        flow_share = lax.psum_scatter(
            lax.dot_general(
                ptdf, inj_low, (((1,), (1,)), ((), ())), preferred_element_type=jnp.float32
            ),
            "buses",
            scatter_dimension=0,
            tiled=True,
        ).T
        balance = lax.psum(balance_term, "buses")
        dual_flow = dual_step(dual_flow, flow_share, SIGMA_FLOW, -limit_share, limit_share)
        price_level = price_level + KAPPA / total_units * balance
        dual_store = dual_step(
            dual_store, forward_cum(stor_bar, HOURS), SIGMA_STORE, low_bound, high_bound
        )
        gen_old, stor_old = (gen_now, stor_now)
        gen_now, stor_now = (gen_next, stor_next)
    return (gen_now, stor_now, price_level, dual_flow, dual_store)


def solution(mesh):
    return jax.shard_map(
        shards,
        mesh=mesh,
        in_specs=(
            P("lines", "buses"),
            P(None, "buses"),
            P(),
            P("lines"),
            P("buses"),
            P("buses"),
            P("buses"),
            P("buses"),
            P(None, "buses"),
            P("buses"),
            P("buses"),
            P("buses"),
            P("buses"),
            P(None, "buses"),
            P(),
            P(None, ("lines", "buses")),
            P(None, "buses"),
        ),
        out_specs=(
            P(None, "buses"),
            P(None, "buses"),
            P(),
            P(None, ("lines", "buses")),
            P(None, "buses"),
        ),
        check_vma=False,
    )
```

profile of v0, /device:TPU:0, one launch (start us, length us, event | category | flops | bytes accessed | tf_op | source)
XLA Modules:
  0.0 343.0 jit_solution(5107921957427476958)
XLA Ops:
  11.1 6.4 %all-to-all-start = ((s32[1,8,32]{2,0,1:T(1,128)}), s32[1,8,32]{2,0,1:T(1,128)S(1)}, u32[]{:S(2)}, u32[]{:S(2)}) async-start(s32[1,8,32]{2,0,1:T(1,128)} %all_to_all.30), calls=%async_computation | async-start | bytes 8192 | tf_op jit(solution)/shard_map/all_to_all | solution.py:70
  18.4 15.0 %all_gather.6 = bf16[384,1024]{1,0:T(8,128)(2,1)S(1)} all-gather(bf16[384,128]{1,0:T(8,128)(2,1)S(1)} %convert_element_type.65), channel_id=1, replica_groups=mesh['lines'=4,'buses'=8] {'buses'}, dimensions={1}, use_global_device_ids=true | all-gather | bytes 884736 | tf_op jit(solution)/shard_map/all_gather | solution.py:91
  37.1 50.5 %all-reduce.3.cloned.1.call-done = bf16[384,1280]{1,0:T(8,128)(2,1)} async-done(((bf16[384,1280]{1,0:T(8,128)(2,1)}), bf16[384,1280]{1,0:T(8,128)(2,1)}) %all-reduce.3.cloned.1.call-update) | async-done | bytes 983056 | tf_op jit(solution)/shard_map/psum | solution.py:93
  90.2 2.7 gather_fusion.1
  93.7 4.6 %all-to-all-start.1 = ((bf16[384,8,32]{0,2,1:T(8,128)(2,1)}), bf16[384,8,32]{0,2,1:T(8,128)(2,1)}, u32[]{:S(2)}, u32[]{:S(2)}) async-start(bf16[384,8,32]{0,2,1:T(8,128)(2,1)} %bitcast.4), calls=%async_computation.1 | async-start | bytes 393216 | tf_op jit(solution)/shard_map/all_to_all | solution.py:95
  100.8 2.9 copy.78
  103.8 3.0 all-to-all-done.1
  115.1 4.0 %all-to-all-start.2 = ((bf16[384,8,32]{0,2,1:T(8,128)(2,1)}), bf16[384,8,32]{0,2,1:T(8,128)(2,1)}, u32[]{:S(2)}, u32[]{:S(2)}) async-start(bf16[384,8,32]{0,2,1:T(8,128)(2,1)} %bitcast.136), calls=%async_computation.2 | async-start | bytes 393216 | tf_op jit(solution)/shard_map/all_to_all | solution.py:120
  119.9 3.1 gather_fusion.3
  124.7 2.5 fusion.53
  129.2 4.7 %scatter_custom_fusion.2 = f32[384,1280]{0,1:T(8,128)} fusion(s32[384]{0:T(512)} %add_reduce_fusion, f32[]{:T(128)} %constant.64.clone.1, f32[384,128]{0,1:T(8,128)S(1)} %copy.77, f32[]{:T(128)} %constant.140, f32[384,256]{0,1:T(8,128)} %bitcast_convert_fusion.4), kind=kCustom, calls=%fused_computation.22 | custom fusion | flops 294912 | bytes 2556928 | tf_op jit(solution)/shard_map/add | solution.py:124
  133.8 4.5 %convolution_bitcast_fusion.1 = f32[1024,384]{0,1:T(8,128)} fusion(bf16[1024,1280]{1,0:T(8,128)(2,1)S(1)} %copy-done, f32[384,1280]{0,1:T(8,128)} %scatter_custom_fusion.2, f32[384,1280]{0,1:T(8,128)} %copy.78), kind=kOutput, calls=%fused_computation.17 | convolution fusion | flops 1007616000 | bytes 8126464 | tf_op jit(solution)/shard_map/dot_general | solution.py:127
  139.3 6.1 %gather_fusion = f32[1024]{0:T(1024)S(1)} fusion(f32[32768]{0:T(1024)S(1)} %copy-done.1, s32[1024]{0:T(1024)S(1)} %fusion.41), kind=kCustom, calls=%fused_computation.6 | custom fusion | bytes 12288 | tf_op jit(solution)/shard_map/jit(_take)/gather | solution.py:72
  145.5 27.4 %reduce-scatter.3.cloned.1.call-done = f32[128,384]{0,1:T(8,128)} async-done(((f32[1024,384]{0,1:T(8,128)}), f32[128,384]{0,1:T(8,128)}) %reduce-scatter.3.cloned.1.call-update) | async-done | bytes 196624 | tf_op jit(solution)/shard_map/reduce_scatter | solution.py:126
  173.9 15.2 %all_gather.7 = bf16[384,1024]{1,0:T(8,128)(2,1)S(1)} all-gather(bf16[384,128]{1,0:T(8,128)(2,1)S(1)} %fusion.38), channel_id=1, replica_groups=mesh['lines'=4,'buses'=8] {'buses'}, dimensions={1}, use_global_device_ids=true | all-gather | bytes 884736 | tf_op jit(solution)/shard_map/all_gather | solution.py:91
  195.7 45.9 %all-reduce.5.cloned.1.call-done = bf16[384,1280]{1,0:T(8,128)(2,1)} async-done(((bf16[384,1280]{1,0:T(8,128)(2,1)}), bf16[384,1280]{1,0:T(8,128)(2,1)}) %all-reduce.5.cloned.1.call-update) | async-done | bytes 983056 | tf_op jit(solution)/shard_map/psum | solution.py:93
  244.1 2.8 gather_fusion.4
  247.7 4.6 %all-to-all-start.3 = ((bf16[384,8,32]{0,2,1:T(8,128)(2,1)}), bf16[384,8,32]{0,2,1:T(8,128)(2,1)}, u32[]{:S(2)}, u32[]{:S(2)}) async-start(bf16[384,8,32]{0,2,1:T(8,128)(2,1)} %bitcast.18), calls=%async_computation.4 | async-start | bytes 393216 | tf_op jit(solution)/shard_map/all_to_all | solution.py:95
  252.3 17.1 %psum.29 = f32[384]{0:T(512)S(1)} all-reduce(f32[384]{0:T(512)S(1)} %add_subtract_fusion.1), channel_id=1, replica_groups=mesh['lines'=4,'buses'=8] {'buses'}, use_global_device_ids=true, to_apply=%region_9.13 | all-reduce | flops 384 | bytes 3072 | tf_op jit(solution)/shard_map/psum | solution.py:134
  276.5 4.2 %all-to-all-start.4 = ((bf16[384,8,32]{0,2,1:T(8,128)(2,1)}), bf16[384,8,32]{0,2,1:T(8,128)(2,1)}, u32[]{:S(2)}, u32[]{:S(2)}) async-start(bf16[384,8,32]{0,2,1:T(8,128)(2,1)} %bitcast.135), calls=%async_computation.5 | async-start | bytes 393216 | tf_op jit(solution)/shard_map/all_to_all | solution.py:120
  290.6 4.7 %scatter_custom_fusion.4 = f32[384,1280]{0,1:T(8,128)} fusion(s32[384]{0:T(512)} %add_reduce_fusion, f32[]{:T(128)} %constant.64.clone.1, f32[384,128]{0,1:T(8,128)S(1)} %copy.86, f32[]{:T(128)} %constant.140, f32[384,256]{0,1:T(8,128)} %bitcast_convert_fusion.2), kind=kCustom, calls=%fused_computation.20 | custom fusion | flops 294912 | bytes 2556928 | tf_op jit(solution)/shard_map/add | solution.py:124
  295.3 4.5 %convolution_bitcast_fusion = f32[1024,384]{0,1:T(8,128)} fusion(bf16[1024,1280]{1,0:T(8,128)(2,1)S(1)} %copy-done, f32[384,1280]{0,1:T(8,128)} %scatter_custom_fusion.4, f32[384,1280]{0,1:T(8,128)} %copy.78), kind=kOutput, calls=%fused_computation.16 | convolution fusion | flops 1007616000 | bytes 8126464 | tf_op jit(solution)/shard_map/dot_general | solution.py:127
  303.2 16.8 %psum.31 = f32[384]{0:T(512)S(1)} all-reduce(f32[384]{0:T(512)S(1)} %add_subtract_fusion), channel_id=1, replica_groups=mesh['lines'=4,'buses'=8] {'buses'}, use_global_device_ids=true, to_apply=%region_18.22 | all-reduce | flops 384 | bytes 3072 | tf_op jit(solution)/shard_map/psum | solution.py:134
  320.6 14.0 %reduce-scatter.5.cloned.1.call-done = f32[128,384]{0,1:T(8,128)} async-done(((f32[1024,384]{0,1:T(8,128)}), f32[128,384]{0,1:T(8,128)}) %reduce-scatter.5.cloned.1.call-update) | async-done | bytes 196624 | tf_op jit(solution)/shard_map/reduce_scatter | solution.py:126
  (174 shorter events, 61.4 us)
Async XLA Ops:
  7.2 26.3 %copy-start = (bf16[1024,1280]{1,0:T(8,128)(2,1)S(1)}, bf16[1024,1280]{1,0:T(8,128)(2,1)}, u32[]{:S(2)}) copy-start(bf16[1024,1280]{1,0:T(8,128)(2,1)} %param.23) | copy-start | bytes 7864324
  9.0 100.4 %copy-start.16 = (pred[256]{0:T(512)(128)(4,1)}, pred[256]{0:T(512)(128)(4,1)S(1)}, u32[]{:S(2)}) copy-start(pred[256]{0:T(512)(128)(4,1)S(1)} %get-tuple-element.33) | copy-start | bytes 772
  9.0 102.3 %copy-start.22 = (s32[256]{0:T(256)}, s32[256]{0:T(256)S(1)}, u32[]{:S(2)}) copy-start(s32[256]{0:T(256)S(1)} %get-tuple-element.34) | copy-start | bytes 3076
  11.1 25.9 %all-to-all-start = ((s32[1,8,32]{2,0,1:T(1,128)}), s32[1,8,32]{2,0,1:T(1,128)S(1)}, u32[]{:S(2)}, u32[]{:S(2)}) async-start(s32[1,8,32]{2,0,1:T(1,128)} %all_to_all.30), calls=%async_computation | async-start | bytes 8192 | tf_op jit(solution)/shard_map/all_to_all | solution.py:70
  17.4 70.2 %all-reduce.3.cloned.1.call-start = ((), (), s32[]{:S(2)}) async-start(), calls=%async_computation.7 | async-start | bytes 1966080 | tf_op jit(solution)/shard_map/psum | solution.py:93
  37.0 87.7 %copy-start.25 = (pred[128]{0:T(512)(128)(4,1)}, pred[128]{0:T(512)(128)(4,1)S(1)}, u32[]{:S(2)}) copy-start(pred[128]{0:T(512)(128)(4,1)S(1)} %get-tuple-element.35) | copy-start | bytes 388
  37.1 55.8 %copy-start.11 = (s32[1024]{0:T(1024)}, s32[1024]{0:T(1024)S(1)}, u32[]{:S(2)}) copy-start(s32[1024]{0:T(1024)S(1)} %pad_clamp_fusion.2) | copy-start | bytes 12292
  37.1 55.8 %copy-start.30 = (pred[256]{0:T(512)(128)(4,1)}, pred[256]{0:T(512)(128)(4,1)S(1)}, u32[]{:S(2)}) copy-start(pred[256]{0:T(512)(128)(4,1)S(1)} %compare_and_fusion.2) | copy-start | bytes 772
  93.7 13.0 %all-to-all-start.1 = ((bf16[384,8,32]{0,2,1:T(8,128)(2,1)}), bf16[384,8,32]{0,2,1:T(8,128)(2,1)}, u32[]{:S(2)}, u32[]{:S(2)}) async-start(bf16[384,8,32]{0,2,1:T(8,128)(2,1)} %bitcast.4), calls=%async_computation.1 | async-start | bytes 393216 | tf_op jit(solution)/shard_map/all_to_all | solution.py:95
  98.3 26.4 %copy-start.27 = (f32[128]{0:T(128)}, f32[128]{0:T(128)S(1)}, u32[]{:S(2)}) copy-start(f32[128]{0:T(128)S(1)} %broadcast_multiply_fusion.2) | copy-start | bytes 1540
  111.3 11.7 %copy-start.2 = (f32[384,256]{0,1:T(8,128)}, f32[384,256]{0,1:T(8,128)S(1)}, u32[]{:S(2)}) copy-start(f32[384,256]{0,1:T(8,128)S(1)} %get-tuple-element.32) | copy-start | bytes 1179652
  115.1 12.3 %all-to-all-start.2 = ((bf16[384,8,32]{0,2,1:T(8,128)(2,1)}), bf16[384,8,32]{0,2,1:T(8,128)(2,1)}, u32[]{:S(2)}, u32[]{:S(2)}) async-start(bf16[384,8,32]{0,2,1:T(8,128)(2,1)} %bitcast.136), calls=%async_computation.2 | async-start | bytes 393216 | tf_op jit(solution)/shard_map/all_to_all | solution.py:120
  119.2 53.8 %reduce-scatter.3.cloned.1.call-start = ((), (), s32[]{:S(2)}) async-start(), calls=%async_computation.8 | async-start | bytes 1769472 | tf_op jit(solution)/shard_map/reduce_scatter | solution.py:126
  138.4 103.1 %all-reduce.5.cloned.1.call-start = ((), (), s32[]{:S(2)}) async-start(), calls=%async_computation.9 | async-start | bytes 1966080 | tf_op jit(solution)/shard_map/psum | solution.py:93
  139.3 33.7 %copy-start.3 = (f32[384,128]{1,0:T(8,128)S(1)}, f32[384,128]{1,0:T(8,128)}, u32[]{:S(2)}) copy-start(f32[384,128]{1,0:T(8,128)} %param.38) | copy-start | bytes 589828
  193.0 48.5 %copy-start.32 = (pred[384]{0:T(512)(128)(4,1)}, pred[384]{0:T(512)(128)(4,1)S(1)}, u32[]{:S(2)}) copy-start(pred[384]{0:T(512)(128)(4,1)S(1)} %fusion.42) | copy-start | bytes 1156
  193.1 48.5 %copy-start.34 = (f32[128]{0:T(128)}, f32[128]{0:T(128)S(1)}, u32[]{:S(2)}) copy-start(f32[128]{0:T(128)S(1)} %get-tuple-element.43) | copy-start | bytes 1540
  195.7 51.2 %copy-start.31 = (pred[256]{0:T(512)(128)(4,1)S(1)}, pred[256]{0:T(512)(128)(4,1)}, u32[]{:S(2)}) copy-start(pred[256]{0:T(512)(128)(4,1)} %copy-done.30) | copy-start | bytes 772
  247.7 21.8 %all-to-all-start.3 = ((bf16[384,8,32]{0,2,1:T(8,128)(2,1)}), bf16[384,8,32]{0,2,1:T(8,128)(2,1)}, u32[]{:S(2)}, u32[]{:S(2)}) async-start(bf16[384,8,32]{0,2,1:T(8,128)(2,1)} %bitcast.18), calls=%async_computation.4 | async-start | bytes 393216 | tf_op jit(solution)/shard_map/all_to_all | solution.py:95
  276.5 10.2 %copy-start.28 = (f32[128]{0:T(128)S(1)}, f32[128]{0:T(128)}, u32[]{:S(2)}) copy-start(f32[128]{0:T(128)} %copy-done.27) | copy-start | bytes 1540
  276.5 10.2 %copy-start.29 = (f32[128]{0:T(128)S(1)}, f32[128]{0:T(128)}, u32[]{:S(2)}) copy-start(f32[128]{0:T(128)} %neg.12) | copy-start | bytes 1540
  276.5 12.5 %all-to-all-start.4 = ((bf16[384,8,32]{0,2,1:T(8,128)(2,1)}), bf16[384,8,32]{0,2,1:T(8,128)(2,1)}, u32[]{:S(2)}, u32[]{:S(2)}) async-start(bf16[384,8,32]{0,2,1:T(8,128)(2,1)} %bitcast.135), calls=%async_computation.5 | async-start | bytes 393216 | tf_op jit(solution)/shard_map/all_to_all | solution.py:120
  280.6 54.0 %reduce-scatter.5.cloned.1.call-start = ((), (), s32[]{:S(2)}) async-start(), calls=%async_computation.10 | async-start | bytes 1769472 | tf_op jit(solution)/shard_map/reduce_scatter | solution.py:126
  299.8 34.8 %copy-start.4 = (f32[384,128]{1,0:T(8,128)S(1)}, f32[384,128]{1,0:T(8,128)}, u32[]{:S(2)}) copy-start(f32[384,128]{1,0:T(8,128)} %param.38) | copy-start | bytes 589828
  (27 other events, 118.0 us)
Sparse Core Ops, SparseCore 0:
  35.8 51.8 all-reduce.2
  138.5 34.3 reduce-scatter.2
  191.4 50.0 all-reduce.4
  300.0 34.5 reduce-scatter.4
where the time goes:
time: 344 us; the launch traced here: 343 us
  waiting for transfers between devices  141 us (41%)
  blocking collectives  64.1 us (19%)
  other arithmetic  44.4 us (13%)
  local copies, waits for them, and re-layouts  41.6 us (12%)
  starting transfers between devices  23.9 us (7%)
  between operations  14.3 us (4%)
  matrix products  13.4 us (4%)
    psum x2, waiting for transfers between devices, shards(): lax.psum(partial_value.astype(jnp.bfloat16), 'lines').astype(jnp.float32)  96.4 us
    reduce_scatter x2, waiting for transfers between devices, shards(): lax.psum_scatter(lax.dot_general(ptdf, inj_low, (((1,), (1,)), ((), ())),...  41.5 us
    psum x2, blocking collectives, shards(): balance = lax.psum(balance_term, 'buses')  34 us
    all_gather x2, blocking collectives, shards(): lax.all_gather(dual_flow.astype(jnp.bfloat16), 'buses', axis=1, tiled=True)  30.2 us
    add x2, other arithmetic, shards(): injection = empty.at[:, arrived_bus].add(received) + stor_inject - load  9.35 us
    all_to_all x2, starting transfers between devices, shards(): lax.all_to_all(jnp.take(bus_price, arrived_bus, axis=1).astype(jnp.bfloat...  9.21 us
    dot_general x2, matrix products, shards(): lax.dot_general(ptdf, inj_low, (((1,), (1,)), ((), ())), preferred_elemen...  9.07 us
    all_to_all x2, starting transfers between devices, shards(): lax.all_to_all(slotted.astype(jnp.bfloat16), 'buses', split_axis=1, conca...  8.18 us
  transfers between devices with their start and end apart: 9, of which 7 were waited for; matrix products, arithmetic and copies ran while one was open for 11% of the time, Pallas kernels for 0%

commit v1 on v0

v1 whole, which is shorter than its diff:
```python
import functools
import jax
import jax.numpy as jnp
from jax import lax
from jax.experimental import pallas as pl
from jax.experimental.pallas import tpu as pltpu
from jax.sharding import PartitionSpec as P

HOURS = 24
TAU = 0.25
SIGMA_FLOW = 4.0
SIGMA_STORE = 0.25
KAPPA = 1.0
THETA = 0.5

F32 = jnp.float32
BF16 = jnp.bfloat16
MESH = pl.DeviceIdType.MESH
HIGHEST = lax.Precision.HIGHEST


def nt(a, b, precision=None):
    return lax.dot_general(
        a, b, (((1,), (1,)), ((), ())), preferred_element_type=F32, precision=precision
    )


def nn(a, b, precision=None):
    return lax.dot_general(
        a, b, (((1,), (0,)), ((), ())), preferred_element_type=F32, precision=precision
    )


def iota(shape, dim):
    return lax.broadcasted_iota(jnp.int32, shape, dim)


def eye(n):
    return iota((n, n), 0) == iota((n, n), 1)


def flipped(x):
    return nt(eye(x.shape[1]).astype(F32), x, HIGHEST)


def to_column(row):
    n = row.shape[1]
    return jnp.sum(jnp.where(eye(n), row, 0.0), axis=1, keepdims=True)


def to_row(column):
    n = column.shape[0]
    return jnp.sum(jnp.where(eye(n), column, 0.0), axis=0, keepdims=True)


def remote(src, dst, send_sem, recv_sem, target):
    return pltpu.make_async_remote_copy(
        src_ref=src,
        dst_ref=dst,
        send_sem=send_sem,
        recv_sem=recv_sem,
        device_id=target,
        device_id_type=MESH,
    )


def kernel(
    lines_n,
    buses_n,
    slots,
    gen_bus,
    mu_in,
    ratings,
    line_index,
    gen_quad,
    gen_lin,
    gen_max,
    gen_start,
    stor_bus,
    stor_quad,
    stor_rate,
    stor_energy,
    stor_start,
    lam_in,
    omega_in,
    ptdf_hbm,
    load_hbm,
    gen_out,
    stor_out,
    lam_out,
    mu_out,
    omega_out,
    ptdf,
    load,
    load_low,
    load_flow,
    gen_all,
    a_send,
    a_recv,
    a_t,
    a_n,
    dual_all,
    price_part,
    price_recv,
    price_all,
    bar_low,
    flow_part,
    pair_recv,
    line_part,
    line_recv,
    bal_send,
    bal_recv,
    in_sem,
    idx_sem,
    a_sem,
    ag_sem,
    fwd_sem,
    pr_sem,
    pg_sem,
    pair_sem,
    line_sem,
    bal_sem,
):
    rows = load.shape[0]
    line_count, bus_count = ptdf.shape
    gens = gen_bus.shape[1]
    stors = stor_bus.shape[1]
    units = gens + stors
    share = mu_in.shape[1]
    chips = buses_n // 2
    width = buses_n * slots
    piece = units // lines_n
    i = lax.axis_index("lines")
    j = lax.axis_index("buses")
    z = j // 2
    c = j % 2
    partner = (i, z * 2 + (1 - c))

    load_copy = pltpu.make_async_copy(load_hbm, load, in_sem.at[0])
    ptdf_copy = pltpu.make_async_copy(ptdf_hbm, ptdf, in_sem.at[1])
    load_copy.start()
    ptdf_copy.start()

    barrier = pltpu.get_barrier_semaphore()
    for off in range(1, buses_n):
        pl.semaphore_signal(
            barrier, inc=1, device_id=(i, lax.rem(j + off, buses_n)), device_id_type=MESH
        )
    for off in range(1, lines_n):
        pl.semaphore_signal(
            barrier, inc=1, device_id=(lax.rem(i + off, lines_n), j), device_id_type=MESH
        )

    gen_all[j] = gen_bus[...]
    mu = flipped(mu_in[...])
    dual_all[0, j] = mu.astype(BF16)
    pl.semaphore_wait(barrier, buses_n + lines_n - 2)

    started = []

    def go(copy):
        copy.start()
        started.append(copy)
        return copy

    idx_copies = []
    for off in range(1, buses_n):
        idx_copies.append(
            go(
                remote(
                    gen_bus,
                    gen_all.at[j],
                    idx_sem.at[0, off],
                    idx_sem.at[1, off],
                    (i, lax.rem(j + off, buses_n)),
                )
            )
        )

    def gather_start(k):
        mine = dual_all.at[k, j]
        copies = [go(remote(mine, mine, ag_sem.at[k, 0, 0], ag_sem.at[k, 1, 0], partner))]
        for off in range(1, chips):
            copies.append(
                go(
                    remote(
                        mine,
                        mine,
                        ag_sem.at[k, 0, off],
                        ag_sem.at[k, 1, off],
                        (i, lax.rem(z + off, chips) * 2 + c),
                    )
                )
            )
        return copies

    def gather_finish(k, copies):
        forwards = []
        for off in range(1, chips):
            copies[off].wait_recv()
            slot = dual_all.at[k, lax.rem(z - off + chips, chips) * 2 + c]
            forwards.append(
                go(remote(slot, slot, fwd_sem.at[k, 0, off], fwd_sem.at[k, 1, off], partner))
            )
        copies[0].wait_recv()
        for copy in forwards:
            copy.wait_recv()

    gather = gather_start(0)

    load_copy.wait()
    load_value = load[...]
    load_total = jnp.sum(load_value, axis=1, keepdims=True)
    load_low[...] = load_value.astype(BF16)
    lam = to_column(lam_in[...])
    wanted = jnp.sum(
        jnp.where(iota((buses_n, share), 0) == j, line_index[...].astype(F32), 0.0),
        axis=0,
        keepdims=True,
    )
    wanted = to_column(wanted).astype(jnp.int32)
    lanes = ratings.shape[1]
    high_hit = (iota((share, ratings.shape[0]), 1) == wanted // lanes).astype(F32)
    rated = nn(high_hit, ratings[...], HIGHEST)
    limit = jnp.sum(
        jnp.where(iota((share, lanes), 1) == wanted % lanes, rated, 0.0), axis=1, keepdims=True
    )
    hour = iota((rows, 1), 0) % HOURS
    half_energy = 0.5 * stor_energy[...]
    high_bound = jnp.where(hour == HOURS - 1, 0.0, half_energy)
    row_id, col_id = (iota((rows, rows), 0), iota((rows, rows), 1))
    same = row_id // HOURS == col_id // HOURS
    later = jnp.where(same & (col_id >= row_id), 1.0, 0.0)
    earlier = jnp.where(same & (col_id <= row_id), 1.0, 0.0)

    for copy in idx_copies:
        copy.wait_recv()
    ids = jnp.concatenate([gen_all[a] for a in range(buses_n)], axis=0)
    ids = flipped(ids.astype(F32)).astype(jnp.int32)
    local = ids - j * bus_count
    hit = (local >= 0) & (local < bus_count)
    upto = (iota((gens, gens), 1) <= iota((gens, gens), 0)).astype(BF16)
    rank = nn(upto, hit.astype(BF16)) - 1.0
    rank = jnp.where(hit, rank, 512.0)
    local = jnp.where(hit, local, 0)
    spread = (iota((buses_n, width), 1) // slots == iota((buses_n, width), 0)).astype(BF16)
    rank_wide = nn(rank.astype(BF16), spread)
    high_wide = nn((local // 128).astype(BF16), spread)
    low_wide = nn((local % 128).astype(BF16), spread)
    taken = rank_wide == (iota((gens, width), 1) % slots).astype(F32)
    slot_bus = jnp.sum(jnp.where(taken, high_wide * 128.0 + low_wide + 1.0, 0.0), axis=0, keepdims=True)
    slot_bus = to_column(slot_bus).astype(jnp.int32) - 1
    slot_hit = (iota((width, bus_count), 1) == slot_bus).astype(BF16)
    stor_column = to_column(stor_bus[...].astype(F32)).astype(jnp.int32)
    stor_hit = (iota((stors, bus_count), 1) == stor_column).astype(BF16)
    ptdf_copy.wait()
    tile = 128

    def columns_step(t, carry):
        at = pl.multiple_of(t * tile, tile)
        block = ptdf[pl.ds(at, tile), :]
        a_send[:, :, pl.ds(at, tile)] = nt(slot_hit, block).astype(BF16).reshape(buses_n, slots, tile)
        return carry

    lax.fori_loop(0, line_count // tile, columns_step, 0)
    a_recv[j] = a_send[j]
    a_copies = []
    for off in range(1, buses_n):
        to = lax.rem(j + off, buses_n)
        a_copies.append(
            go(remote(a_send.at[to], a_recv.at[j], a_sem.at[0, off], a_sem.at[1, off], (i, to)))
        )

    def load_step(t, carry):
        at = pl.multiple_of(t * tile, tile)
        block = ptdf[pl.ds(at, tile), :]
        load_flow[pl.ds(at, tile), :] = nt(block, load_low[...])
        stor_block = nt(block, stor_hit)
        a_n[pl.ds(at, tile), gens:] = stor_block.astype(BF16)
        a_t[gens:, pl.ds(at, tile)] = stor_block.T.astype(BF16)
        return carry

    lax.fori_loop(0, line_count // tile, load_step, 0)
    own = jnp.sum(jnp.where(iota((gens, buses_n), 1) == j, ids, 0), axis=1, keepdims=True)
    target = own // bus_count
    target_hit = iota((gens, buses_n), 1) == target
    own_rank = nn(upto, target_hit.astype(BF16))
    own_rank = jnp.sum(jnp.where(target_hit, own_rank, 0.0), axis=1, keepdims=True).astype(jnp.int32) - 1
    place = (iota((gens, width), 1) == target * slots + own_rank).astype(BF16)

    gather_finish(0, gather)
    for copy in a_copies:
        copy.wait_recv()

    def place_step(t, carry):
        at = pl.multiple_of(t * tile, tile)
        block = nn(place, a_recv[:, :, pl.ds(at, tile)].reshape(width, tile))
        a_t[:gens, pl.ds(at, tile)] = block.astype(BF16)
        a_n[pl.ds(at, tile), :gens] = block.T.astype(BF16)
        return carry

    lax.fori_loop(0, line_count // tile, place_step, 0)

    gen_now, stor_now = (gen_start[...], stor_start[...])
    gen_old, stor_old = (gen_now, stor_now)
    omega = omega_in[...]
    total_units = units * buses_n
    for k in range(2):
        if k == 0:
            gen_mid, stor_mid = (gen_now, stor_now)
        else:
            gen_mid = gen_now + THETA * (gen_now - gen_old)
            stor_mid = stor_now + THETA * (stor_now - stor_old)
        duals = dual_all[k].reshape(line_count, rows)
        copies = []
        for off in range(1, lines_n + 1):
            to = lax.rem(i + off, lines_n)
            at = pl.multiple_of(to * piece, piece)
            value = nn(a_t[pl.ds(at, piece), :], duals)
            if off == lines_n:
                total = value
                break
            price_part[k, off] = value.astype(BF16)
            copies.append(
                go(
                    remote(
                        price_part.at[k, off],
                        price_recv.at[k, off],
                        pr_sem.at[k, 0, off],
                        pr_sem.at[k, 1, off],
                        (to, j),
                    )
                )
            )
        back = nn(later, omega, HIGHEST)
        for off in range(1, lines_n):
            copies[off - 1].wait_recv()
            total = total + price_recv[k, off].astype(F32)
        price_all[k, i] = total.astype(BF16)
        copies = []
        for off in range(1, lines_n):
            copies.append(
                go(
                    remote(
                        price_all.at[k, i],
                        price_all.at[k, i],
                        pg_sem.at[k, 0, off],
                        pg_sem.at[k, 1, off],
                        (lax.rem(i + off, lines_n), j),
                    )
                )
            )
        for copy in copies:
            copy.wait_recv()
        price = price_all[k].reshape(units, rows).astype(F32).T

        gen_grad = 2.0 * gen_quad[...] * gen_mid + gen_lin[...] + lam + price[:, :gens]
        gen_next = jnp.clip(gen_mid - TAU * gen_grad, 0.0, gen_max[...])
        stor_grad = 2.0 * stor_quad[...] * stor_mid + lam + price[:, gens:] + back
        stor_next = jnp.clip(stor_mid - TAU * stor_grad, -stor_rate[...], stor_rate[...])
        gen_bar = 2.0 * gen_next - gen_now
        stor_bar = 2.0 * stor_next - stor_now
        bar_low[:, :gens] = gen_bar.astype(BF16)
        bar_low[:, gens:] = stor_bar.astype(BF16)

        def flow_step(chip, carry, want):
            at = pl.multiple_of((chip * 2 + want) * share, share)
            value = nt(a_n[pl.ds(at, share), :], bar_low[...]) - load_flow[pl.ds(at, share), :]
            flow_part[k, want, chip] = value.astype(BF16)
            return carry

        lax.fori_loop(0, chips, functools.partial(flow_step, want=1 - c), 0)
        pair_copy = go(
            remote(
                flow_part.at[k, 1 - c],
                pair_recv.at[k],
                pair_sem.at[k, 0],
                pair_sem.at[k, 1],
                partner,
            )
        )
        lax.fori_loop(0, chips, functools.partial(flow_step, want=c), 0)
        pair_copy.wait_recv()
        copies = []
        for off in range(1, chips):
            to = lax.rem(z + off, chips)
            line_part[k, off] = (flow_part[k, c, to].astype(F32) + pair_recv[k, to].astype(F32)).astype(BF16)
            copies.append(
                go(
                    remote(
                        line_part.at[k, off],
                        line_recv.at[k, off],
                        line_sem.at[k, 0, off],
                        line_sem.at[k, 1, off],
                        (i, to * 2 + c),
                    )
                )
            )
        balance = (
            jnp.sum(gen_bar, axis=1, keepdims=True)
            + jnp.sum(stor_bar, axis=1, keepdims=True)
            - load_total
        )
        balance = to_row(balance)
        bal_send[k] = balance
        bal_copies = []
        for off in range(1, buses_n):
            bal_copies.append(
                go(
                    remote(
                        bal_send.at[k],
                        bal_recv.at[k, j],
                        bal_sem.at[k, 0, off],
                        bal_sem.at[k, 1, off],
                        (i, lax.rem(j + off, buses_n)),
                    )
                )
            )
        bal_recv[k, j] = balance
        charge = nn(earlier, stor_bar, HIGHEST)
        shifted = omega + SIGMA_STORE * charge
        omega = shifted - SIGMA_STORE * jnp.clip(shifted / SIGMA_STORE, -high_bound, high_bound)
        flow = flow_part[k, c, z].astype(F32) + pair_recv[k, z].astype(F32)
        for off in range(1, chips):
            copies[off - 1].wait_recv()
            flow = flow + line_recv[k, off].astype(F32)
        shifted = mu + SIGMA_FLOW * flow
        mu = shifted - SIGMA_FLOW * jnp.clip(shifted / SIGMA_FLOW, -limit, limit)
        if k == 0:
            dual_all[1, j] = mu.astype(BF16)
            gather = gather_start(1)
        gen_old, stor_old = (gen_now, stor_now)
        gen_now, stor_now = (gen_next, stor_next)
        for copy in bal_copies:
            copy.wait_recv()
        balance = bal_recv[k, 0]
        for a in range(1, buses_n):
            balance = balance + bal_recv[k, a]
        lam = lam + (KAPPA / total_units) * to_column(balance)
        if k == 0:
            gather_finish(1, gather)

    gen_out[...] = gen_now
    stor_out[...] = stor_now
    lam_out[...] = to_row(lam)
    mu_out[...] = flipped(mu)
    omega_out[...] = omega
    for copy in started:
        copy.wait_send()


def shards(
    ptdf,
    load,
    ratings,
    line_index,
    gen_bus,
    gen_quad,
    gen_lin,
    gen_max,
    gen_start,
    stor_bus,
    stor_quad,
    stor_rate,
    stor_energy,
    stor_start,
    lam_start,
    mu_start,
    omega_start,
):
    lines_n = lax.axis_size("lines")
    buses_n = lax.axis_size("buses")
    rows, bus_count = load.shape
    line_count = ptdf.shape[0]
    gens = gen_bus.shape[0]
    stors = stor_bus.shape[0]
    units = gens + stors
    share = line_count // buses_n
    chips = buses_n // 2
    piece = units // lines_n
    slots = max(8, (gens + buses_n - 1) // buses_n)
    slots = (slots + 15) // 16 * 16
    width = buses_n * slots
    vmem = pl.BlockSpec(memory_space=pltpu.VMEM)
    hbm = pl.BlockSpec(memory_space=pl.ANY)
    dma = pltpu.SemaphoreType.DMA
    outs = pl.pallas_call(
        functools.partial(kernel, lines_n, buses_n, slots),
        out_shape=(
            jax.ShapeDtypeStruct((rows, gens), F32),
            jax.ShapeDtypeStruct((rows, stors), F32),
            jax.ShapeDtypeStruct((1, rows), F32),
            jax.ShapeDtypeStruct((rows, share), F32),
            jax.ShapeDtypeStruct((rows, stors), F32),
        ),
        in_specs=[vmem] * 15 + [hbm] * 2,
        out_specs=(vmem,) * 5,
        scratch_shapes=[
            pltpu.VMEM((line_count, bus_count), BF16),
            pltpu.VMEM((rows, bus_count), F32),
            pltpu.VMEM((rows, bus_count), BF16),
            pltpu.VMEM((line_count, rows), F32),
            pltpu.VMEM((buses_n, 1, gens), jnp.int32),
            pltpu.VMEM((buses_n, slots, line_count), BF16),
            pltpu.VMEM((buses_n, slots, line_count), BF16),
            pltpu.VMEM((units, line_count), BF16),
            pltpu.VMEM((line_count, units), BF16),
            pltpu.VMEM((2, buses_n, share, rows), BF16),
            pltpu.VMEM((2, lines_n, piece, rows), BF16),
            pltpu.VMEM((2, lines_n, piece, rows), BF16),
            pltpu.VMEM((2, lines_n, piece, rows), BF16),
            pltpu.VMEM((rows, units), BF16),
            pltpu.VMEM((2, 2, chips, share, rows), BF16),
            pltpu.VMEM((2, chips, share, rows), BF16),
            pltpu.VMEM((2, chips, share, rows), BF16),
            pltpu.VMEM((2, chips, share, rows), BF16),
            pltpu.VMEM((2, 1, rows), F32),
            pltpu.VMEM((2, buses_n, 1, rows), F32),
            dma((2,)),
            dma((2, buses_n)),
            dma((2, buses_n)),
            dma((2, 2, chips)),
            dma((2, 2, chips)),
            dma((2, 2, lines_n)),
            dma((2, 2, lines_n)),
            dma((2, 2)),
            dma((2, 2, chips)),
            dma((2, 2, buses_n)),
        ],
        compiler_params=pltpu.CompilerParams(
            collective_id=0, has_side_effects=True, vmem_limit_bytes=60 * 1024 * 1024
        ),
    )(
        gen_bus[None, :],
        mu_start,
        ratings.reshape(-1, 128),
        line_index.reshape(buses_n, share),
        gen_quad[None, :],
        gen_lin[None, :],
        gen_max[None, :],
        gen_start,
        stor_bus[None, :],
        stor_quad[None, :],
        stor_rate[None, :],
        stor_energy[None, :],
        stor_start,
        lam_start[None, :],
        omega_start,
        ptdf,
        load,
    )
    return (outs[0], outs[1], outs[2].reshape(rows), outs[3], outs[4])


def solution(mesh):
    return jax.shard_map(
        shards,
        mesh=mesh,
        in_specs=(
            P("lines", "buses"),
            P(None, "buses"),
            P(),
            P("lines"),
            P("buses"),
            P("buses"),
            P("buses"),
            P("buses"),
            P(None, "buses"),
            P("buses"),
            P("buses"),
            P("buses"),
            P("buses"),
            P(None, "buses"),
            P(),
            P(None, ("lines", "buses")),
            P(None, "buses"),
        ),
        out_specs=(
            P(None, "buses"),
            P(None, "buses"),
            P(),
            P(None, ("lines", "buses")),
            P(None, "buses"),
        ),
        check_vma=False,
    )
```

time: 344 us -> 103 us (0.30)
  waiting for transfers between devices: 141 us -> 0 us
  Pallas kernels: 0 us -> 93.1 us
  blocking collectives: 64.1 us -> 0 us
  other arithmetic: 44.4 us -> 1.26 us
  local copies, waits for them, and re-layouts: 41.6 us -> 7.86 us
  starting transfers between devices: 23.9 us -> 0 us
  between operations: 14.3 us -> 0.64 us
  matrix products: 13.4 us -> 0 us
    psum x2 -> x0, waiting for transfers between devices: 96.4 us -> none  [shards(): lax.psum(partial_value.astype(jnp.bfloat16), 'lines').astype(jnp.float32)]
    pallas_call x0 -> x1, Pallas kernels: none -> 93.1 us  [shards(): pl.pallas_call(functools.partial(kernel, lines_n, buses_n, slots), out_sh...]
    reduce_scatter x2 -> x0, waiting for transfers between devices: 41.5 us -> none  [shards(): lax.psum_scatter(lax.dot_general(ptdf, inj_low, (((1,), (1,)), ((), ())),...]
    psum x2 -> x0, blocking collectives: 34 us -> none  [shards(): balance = lax.psum(balance_term, 'buses')]
    all_gather x2 -> x0, blocking collectives: 30.2 us -> none  [shards(): lax.all_gather(dual_flow.astype(jnp.bfloat16), 'buses', axis=1, tiled=True)]
    all_to_all x5 -> x0, starting transfers between devices: 23.7 us -> none  [the longest x2 9.21 us: shards(): lax.all_to_all(jnp.take(bus_price, arrived_bus, axis=1).astype(jnp.bfloat...]
    gather x9 -> x0, local copies, waits for them, and re-layouts: 23.4 us -> none  [the longest x4 8.11 us: shards(): stor_price = jnp.take(bus_price, stor_bus, axis=1)]
    dot_general x4 -> x0, matrix products: 13.4 us -> none  [the longest x2 9.07 us: shards(): lax.dot_general(ptdf, inj_low, (((1,), (1,)), ((), ())), preferred_elemen...]
  transfers between devices with their start and end apart: 9 -> 0, of which waited for: 7 -> 0; matrix products, arithmetic and copies ran while one was open for 11% -> 0% of each run, Pallas kernels for 0% -> 0%
where the time goes in v1:
time: 103 us
  Pallas kernels  93.1 us (90%)
  local copies, waits for them, and re-layouts  7.86 us (8%)
  other arithmetic  1.26 us (1%)
    pallas_call x1, Pallas kernels, shards(): pl.pallas_call(functools.partial(kernel, lines_n, buses_n, slots), out_sh...  93.1 us
    unnamed x4, local copies, waits for them, and re-layouts  6.61 us

profile of v1, /device:TPU:0, one launch (start us, length us, event | category | flops | bytes accessed | tf_op | source)
XLA Modules:
  0.0 102.8 jit_solution(13585089521875312959)
XLA Ops:
  0.6 1.2 %broadcast_in_dim.35.lam_in = f32[1,384]{1,0:T(1,128)} reshape(f32[384]{0:T(512)} %param.31) | data formatting | bytes 3072 | tf_op jit(solution)/shard_map/broadcast_in_dim | solution.py:547
  1.9 93.1 %shard_map.200 = (f32[384,256]{1,0:T(8,128)}, f32[384,128]{1,0:T(8,128)}, f32[1,384]{1,0:T(1,128)}, f32[384,128]{1,0:T(8,128)}, f32[384,128]{1,0:T(8,128)}) custom-call(s32[1,256]{1,0:T(1,128)} %bitcast.12, f32[384,128]{1,0:T(8,128)} %mu_in.1, f32[256,128]{1,0:T(8,128)} %bitcast.10, s32[8,128]{1,0:T(8,128)} %bitcast.11, f32[1,256]{1,0:T(1,128)} %bitcast.13, ...), custom_call_target="tpu_custom_call" | custom-call | tf_op jit(solution)/shard_map/pallas_call | solution.py:487
  94.9 1.3 %reduce = f32[384]{0:T(512)} reduce(f32[1,384]{1,0:T(1,128)} %get-tuple-element.12, f32[]{:T(128)} %constant), dimensions={0}, to_apply=%get-tuple-element.12.reduce_sub_computation | reduce | bytes 3076 | tf_op jit(solution)/shard_map/pallas_call | solution.py:487
  96.2 1.8 %copy.26 = f32[384,256]{1,0:T(8,128)} copy(f32[384,256]{1,0:T(8,128)} %get-tuple-element.20) | data formatting | bytes 786432
  98.0 1.6 %copy.27 = f32[384,128]{1,0:T(8,128)} copy(f32[384,128]{1,0:T(8,128)} %get-tuple-element.21) | data formatting | bytes 393216
  99.6 1.6 %copy.28 = f32[384,128]{1,0:T(8,128)} copy(f32[384,128]{1,0:T(8,128)} %get-tuple-element.23) | data formatting | bytes 393216
  101.2 1.6 %copy.29 = f32[384,128]{1,0:T(8,128)} copy(f32[384,128]{1,0:T(8,128)} %get-tuple-element.24) | data formatting | bytes 393216

commit v2 on v1

v2 whole, which is shorter than its diff:
```python
import functools
import jax
import jax.numpy as jnp
from jax import lax
from jax.experimental import pallas as pl
from jax.experimental.pallas import tpu as pltpu
from jax.sharding import PartitionSpec as P

HOURS = 24
TAU = 0.25
SIGMA_FLOW = 4.0
SIGMA_STORE = 0.25
KAPPA = 1.0
THETA = 0.5

F32 = jnp.float32
BF16 = jnp.bfloat16
MESH = pl.DeviceIdType.MESH
HIGHEST = lax.Precision.HIGHEST


def nt(a, b, precision=None):
    return lax.dot_general(
        a, b, (((1,), (1,)), ((), ())), preferred_element_type=F32, precision=precision
    )


def nn(a, b, precision=None):
    return lax.dot_general(
        a, b, (((1,), (0,)), ((), ())), preferred_element_type=F32, precision=precision
    )


def iota(shape, dim):
    return lax.broadcasted_iota(jnp.int32, shape, dim)


def eye(n):
    return iota((n, n), 0) == iota((n, n), 1)


def flipped(x):
    return nt(eye(x.shape[1]).astype(F32), x, HIGHEST)


def to_column(row):
    n = row.shape[1]
    return jnp.sum(jnp.where(eye(n), row, 0.0), axis=1, keepdims=True)


def to_row(column):
    n = column.shape[0]
    return jnp.sum(jnp.where(eye(n), column, 0.0), axis=0, keepdims=True)


def remote(src, dst, send_sem, recv_sem, target):
    return pltpu.make_async_remote_copy(
        src_ref=src,
        dst_ref=dst,
        send_sem=send_sem,
        recv_sem=recv_sem,
        device_id=target,
        device_id_type=MESH,
    )


def kernel(
    lines_n,
    buses_n,
    slots,
    gen_bus,
    mu_in,
    ratings,
    line_index,
    gen_quad,
    gen_lin,
    gen_max,
    gen_start,
    stor_bus,
    stor_quad,
    stor_rate,
    stor_energy,
    stor_start,
    lam_in,
    omega_in,
    ptdf_hbm,
    load_hbm,
    gen_out,
    stor_out,
    lam_out,
    mu_out,
    omega_out,
    ptdf,
    load,
    load_low,
    load_flow,
    gen_all,
    a_send,
    a_recv,
    a_t,
    a_n,
    dual_all,
    price_part,
    price_recv,
    price_all,
    gen_keep,
    stor_keep,
    bar_keep,
    flow_part,
    pair_recv,
    line_part,
    line_recv,
    bal_send,
    bal_recv,
    in_sem,
    idx_sem,
    a_sem,
    ag_sem,
    fwd_sem,
    pr_sem,
    pg_sem,
    pair_sem,
    line_sem,
    bal_sem,
):
    rows = load.shape[0]
    line_count, bus_count = ptdf.shape
    gens = gen_bus.shape[1]
    stors = stor_bus.shape[1]
    units = gens + stors
    share = mu_in.shape[1]
    chips = buses_n // 2
    width = buses_n * slots
    piece = units // lines_n
    i = lax.axis_index("lines")
    j = lax.axis_index("buses")
    z = j // 2
    c = j % 2
    partner = (i, z * 2 + (1 - c))
    chunk = dual_all.shape[-1]
    chunks = rows // chunk

    def cut(n):
        return slice(n * chunk, (n + 1) * chunk)


    load_copy = pltpu.make_async_copy(load_hbm, load, in_sem.at[0])
    ptdf_copy = pltpu.make_async_copy(ptdf_hbm, ptdf, in_sem.at[1])
    load_copy.start()
    ptdf_copy.start()

    barrier = pltpu.get_barrier_semaphore()
    for off in range(1, buses_n):
        pl.semaphore_signal(
            barrier, inc=1, device_id=(i, lax.rem(j + off, buses_n)), device_id_type=MESH
        )
    for off in range(1, lines_n):
        pl.semaphore_signal(
            barrier, inc=1, device_id=(lax.rem(i + off, lines_n), j), device_id_type=MESH
        )

    gen_all[j] = gen_bus[...]
    mu = flipped(mu_in[...])
    for n in range(chunks):
        dual_all[0, n, j] = mu[:, cut(n)].astype(BF16)
    pl.semaphore_wait(barrier, buses_n + lines_n - 2)

    started = []

    def go(copy):
        copy.start()
        started.append(copy)
        return copy

    idx_copies = []
    for off in range(1, buses_n):
        idx_copies.append(
            go(
                remote(
                    gen_bus,
                    gen_all.at[j],
                    idx_sem.at[0, off],
                    idx_sem.at[1, off],
                    (i, lax.rem(j + off, buses_n)),
                )
            )
        )

    def gather_start(k, n):
        mine = dual_all.at[k, n, j]
        copies = []
        for off in range(1, chips):
            copies.append(
                go(
                    remote(
                        mine,
                        mine,
                        ag_sem.at[k, n, 0, off],
                        ag_sem.at[k, n, 1, off],
                        (i, lax.rem(z + off, chips) * 2 + c),
                    )
                )
            )
        copies.append(go(remote(mine, mine, ag_sem.at[k, n, 0, 0], ag_sem.at[k, n, 1, 0], partner)))
        return copies

    def gather_forward(k, n, copies):
        forwards = [copies[-1]]
        for off in range(1, chips):
            copies[off - 1].wait_recv()
            slot = dual_all.at[k, n, lax.rem(z - off + chips, chips) * 2 + c]
            forwards.append(
                go(remote(slot, slot, fwd_sem.at[k, n, 0, off], fwd_sem.at[k, n, 1, off], partner))
            )
        return forwards

    gather = [gather_start(0, n) for n in range(chunks)]

    load_copy.wait()
    load_value = load[...]
    load_total = jnp.sum(load_value, axis=1, keepdims=True)
    load_low[...] = load_value.astype(BF16)
    lam_row = lam_in[...].reshape(1, rows)
    lam = [to_column(lam_row[:, cut(n)]) for n in range(chunks)]
    wanted = jnp.sum(
        jnp.where(iota((buses_n, share), 0) == j, line_index[...].astype(F32), 0.0),
        axis=0,
        keepdims=True,
    )
    wanted = to_column(wanted).astype(jnp.int32)
    lanes = ratings.shape[1]
    high_hit = (iota((share, ratings.shape[0]), 1) == wanted // lanes).astype(F32)
    rated = nn(high_hit, ratings[...], HIGHEST)
    limit = jnp.sum(
        jnp.where(iota((share, lanes), 1) == wanted % lanes, rated, 0.0), axis=1, keepdims=True
    )
    hour = iota((rows, 1), 0) % HOURS
    half_energy = 0.5 * stor_energy[...]
    high_bound = jnp.where(hour == HOURS - 1, 0.0, half_energy)
    row_id, col_id = (iota((rows, rows), 0), iota((rows, rows), 1))
    same = row_id // HOURS == col_id // HOURS
    later = jnp.where(same & (col_id >= row_id), 1.0, 0.0)
    earlier = jnp.where(same & (col_id <= row_id), 1.0, 0.0)

    for copy in idx_copies:
        copy.wait_recv()
    ids = jnp.concatenate([gen_all[a] for a in range(buses_n)], axis=0)
    ids = flipped(ids.astype(F32)).astype(jnp.int32)
    local = ids - j * bus_count
    hit = (local >= 0) & (local < bus_count)
    upto = (iota((gens, gens), 1) <= iota((gens, gens), 0)).astype(BF16)
    rank = nn(upto, hit.astype(BF16)) - 1.0
    rank = jnp.where(hit, rank, 512.0)
    local = jnp.where(hit, local, 0)
    spread = (iota((buses_n, width), 1) // slots == iota((buses_n, width), 0)).astype(BF16)
    rank_wide = nn(rank.astype(BF16), spread)
    high_wide = nn((local // 128).astype(BF16), spread)
    low_wide = nn((local % 128).astype(BF16), spread)
    taken = rank_wide == (iota((gens, width), 1) % slots).astype(F32)
    slot_bus = jnp.sum(jnp.where(taken, high_wide * 128.0 + low_wide + 1.0, 0.0), axis=0, keepdims=True)
    slot_bus = to_column(slot_bus).astype(jnp.int32) - 1
    slot_hit = (iota((width, bus_count), 1) == slot_bus).astype(BF16)
    stor_column = to_column(stor_bus[...].astype(F32)).astype(jnp.int32)
    stor_hit = (iota((stors, bus_count), 1) == stor_column).astype(BF16)
    ptdf_copy.wait()
    tile = 128
    half = line_count // 2
    a_copies = [[], []]
    for h in range(2):

        def columns_step(t, carry):
            at = pl.multiple_of(t * tile, tile)
            block = ptdf[pl.ds(pl.multiple_of(h * half + t * tile, tile), tile), :]
            value = nt(slot_hit, block).astype(BF16)
            a_send[h, :, :, pl.ds(at, tile)] = value.reshape(buses_n, slots, tile)
            return carry

        lax.fori_loop(0, half // tile, columns_step, 0)
        for off in range(1, buses_n):
            to = lax.rem(j + off, buses_n)
            a_copies[h].append(
                go(
                    remote(
                        a_send.at[h, to],
                        a_recv.at[h, j],
                        a_sem.at[h, 0, off],
                        a_sem.at[h, 1, off],
                        (i, to),
                    )
                )
            )
        a_recv[h, j] = a_send[h, j]

    wide = max(tile, 2 * share)
    group = wide // (2 * share)

    def load_step(t, carry):
        at = pl.multiple_of(t * wide, wide)
        block = ptdf[pl.ds(at, wide), :]
        flow_block = nt(block, load_low[...]).reshape(group, 2, share, rows)
        stor_block = nt(block, stor_hit)
        a_t[gens:, pl.ds(at, wide)] = stor_block.T.astype(BF16)
        stor_block = stor_block.astype(BF16).reshape(group, 2, share, stors)
        for w in range(2):
            load_flow[w, pl.ds(t * group, group)] = flow_block[:, w]
            a_n[w, pl.ds(t * group, group), :, gens:] = stor_block[:, w]
        return carry

    lax.fori_loop(0, line_count // wide, load_step, 0)
    own = jnp.sum(jnp.where(iota((gens, buses_n), 1) == j, ids, 0), axis=1, keepdims=True)
    target = own // bus_count
    target_hit = iota((gens, buses_n), 1) == target
    own_rank = nn(upto, target_hit.astype(BF16))
    own_rank = jnp.sum(jnp.where(target_hit, own_rank, 0.0), axis=1, keepdims=True).astype(jnp.int32) - 1
    place = (iota((gens, width), 1) == target * slots + own_rank).astype(BF16)
    back = nn(later, omega_in[...], HIGHEST)

    gather = [gather_forward(0, n, gather[n]) for n in range(chunks)]
    for h in range(2):
        for copy in a_copies[h]:
            copy.wait_recv()

        def place_step(t, carry):
            at = pl.multiple_of(t * wide, wide)
            start = pl.multiple_of(h * half + t * wide, wide)
            block = nn(place, a_recv[h, :, :, pl.ds(at, wide)].reshape(width, wide))
            a_t[:gens, pl.ds(start, wide)] = block.astype(BF16)
            block = block.T.astype(BF16).reshape(group, 2, share, gens)
            for w in range(2):
                a_n[w, pl.ds(h * (half // (2 * share)) + t * group, group), :, :gens] = block[:, w]
            return carry

        lax.fori_loop(0, half // wide, place_step, 0)

    total_units = units * buses_n
    pending = {}
    hold = {"omega": omega_in[...], "back": back, "mu": [mu[:, cut(n)] for n in range(chunks)]}
    gen_hist = {(0, n): gen_start[cut(n), :] for n in range(chunks)}
    stor_hist = {(0, n): stor_start[cut(n), :] for n in range(chunks)}

    def price_stage(k, n):
        for copy in gather[n]:
            copy.wait_recv()
        duals = dual_all[k, n].reshape(line_count, chunk)
        copies = []
        for off in range(1, lines_n + 1):
            to = lax.rem(i + off, lines_n)
            at = pl.multiple_of(to * piece, piece)
            value = nn(a_t[pl.ds(at, piece), :], duals)
            if off == lines_n:
                break
            price_part[k, n, off] = value.astype(BF16)
            copies.append(
                go(
                    remote(
                        price_part.at[k, n, off],
                        price_recv.at[k, n, off],
                        pr_sem.at[k, n, 0, off],
                        pr_sem.at[k, n, 1, off],
                        (to, j),
                    )
                )
            )
        pending[n] = (value, copies)

    def share_stage(k, n):
        total, copies = pending[n]
        for off in range(1, lines_n):
            copies[off - 1].wait_recv()
            total = total + price_recv[k, n, off].astype(F32)
        price_all[k, n, i] = total.astype(BF16)
        copies = []
        for off in range(1, lines_n):
            copies.append(
                go(
                    remote(
                        price_all.at[k, n, i],
                        price_all.at[k, n, i],
                        pg_sem.at[k, n, 0, off],
                        pg_sem.at[k, n, 1, off],
                        (lax.rem(i + off, lines_n), j),
                    )
                )
            )
        pending[n] = copies

    bal_copies = {}

    def take_balance(k, n):
        for copy in bal_copies[n]:
            copy.wait_recv()
        balance = bal_recv[k, n, 0]
        for a in range(1, buses_n):
            balance = balance + bal_recv[k, n, a]
        lam[n] = lam[n] + (KAPPA / total_units) * to_column(balance)

    def update_stage(k, n):
        gen_now, stor_now = (gen_hist[k, n], stor_hist[k, n])
        if k == 0:
            gen_mid, stor_mid = (gen_now, stor_now)
        else:
            take_balance(k - 1, n)
            gen_mid = gen_now + THETA * (gen_now - gen_hist[k - 1, n])
            stor_mid = stor_now + THETA * (stor_now - stor_hist[k - 1, n])
        for copy in pending[n]:
            copy.wait_recv()
        price = price_all[k, n].reshape(units, chunk).astype(F32).T
        gen_grad = 2.0 * gen_quad[...] * gen_mid + gen_lin[...] + lam[n] + price[:, :gens]
        gen_next = jnp.clip(gen_mid - TAU * gen_grad, 0.0, gen_max[...])
        stor_grad = 2.0 * stor_quad[...] * stor_mid + lam[n] + price[:, gens:] + hold["back"][cut(n), :]
        stor_next = jnp.clip(stor_mid - TAU * stor_grad, -stor_rate[...], stor_rate[...])
        gen_bar = 2.0 * gen_next - gen_now
        stor_bar = 2.0 * stor_next - stor_now
        bar_low = jnp.concatenate([gen_bar.astype(BF16), stor_bar.astype(BF16)], axis=1)

        def flow_half(w):
            value = nt(a_n[w].reshape(chips * share, units), bar_low)
            value = value.reshape(chips, share, chunk) - load_flow[w, :, :, cut(n)]
            flow_part[k, n, w] = value.astype(BF16)

        flow_half(1 - c)
        pending[n] = go(
            remote(
                flow_part.at[k, n, 1 - c],
                pair_recv.at[k, n],
                pair_sem.at[k, n, 0],
                pair_sem.at[k, n, 1],
                partner,
            )
        )
        flow_half(c)
        balance = (
            jnp.sum(gen_bar, axis=1, keepdims=True)
            + jnp.sum(stor_bar, axis=1, keepdims=True)
            - load_total[cut(n), :]
        )
        balance = to_row(balance)
        bal_send[k, n] = balance
        bal_recv[k, n, j] = balance
        bal_copies[n] = []
        for off in range(1, buses_n):
            bal_copies[n].append(
                go(
                    remote(
                        bal_send.at[k, n],
                        bal_recv.at[k, n, j],
                        bal_sem.at[k, n, 0, off],
                        bal_sem.at[k, n, 1, off],
                        (i, lax.rem(j + off, buses_n)),
                    )
                )
            )
        if k == 0:
            gen_keep[cut(n), :] = gen_next
            stor_keep[cut(n), :] = stor_next
            gen_hist[1, n] = gen_next
            stor_hist[1, n] = stor_next
        else:
            gen_out[cut(n), :] = gen_next
            stor_out[cut(n), :] = stor_next
        bar_keep[cut(n), :] = stor_bar

    def pair_stage(k, n):
        pending[n].wait_recv()
        copies = []
        for off in range(1, chips):
            to = lax.rem(z + off, chips)
            value = flow_part[k, n, c, to].astype(F32) + pair_recv[k, n, to].astype(F32)
            line_part[k, n, off] = value.astype(BF16)
            copies.append(
                go(
                    remote(
                        line_part.at[k, n, off],
                        line_recv.at[k, n, off],
                        line_sem.at[k, n, 0, off],
                        line_sem.at[k, n, 1, off],
                        (i, to * 2 + c),
                    )
                )
            )
        pending[n] = copies
        if n == chunks - 1:
            charge = nn(earlier, bar_keep[...], HIGHEST)
            shifted = hold["omega"] + SIGMA_STORE * charge
            omega = shifted - SIGMA_STORE * jnp.clip(shifted / SIGMA_STORE, -high_bound, high_bound)
            if k == 0:
                hold["omega"] = omega
                hold["back"] = nn(later, omega, HIGHEST)
            else:
                omega_out[...] = omega

    def dual_stage(k, n):
        flow = flow_part[k, n, c, z].astype(F32) + pair_recv[k, n, z].astype(F32)
        for off in range(1, chips):
            pending[n][off - 1].wait_recv()
            flow = flow + line_recv[k, n, off].astype(F32)
        shifted = hold["mu"][n] + SIGMA_FLOW * flow
        mu = shifted - SIGMA_FLOW * jnp.clip(shifted / SIGMA_FLOW, -limit, limit)
        if k == 0:
            hold["mu"][n] = mu
            dual_all[1, n, j] = mu.astype(BF16)
            gather[n] = gather_start(1, n)
        else:
            mu_out[cut(n), :] = flipped(mu)

    def forward_stage(k, n):
        gather[n] = gather_forward(k, n, gather[n])

    stages = []
    for k in range(2):
        if k:
            stages.append(functools.partial(forward_stage, k))
        for stage in (price_stage, share_stage, update_stage, pair_stage, dual_stage):
            stages.append(functools.partial(stage, k))
    for step in range(len(stages) + chunks - 1):
        for n in range(chunks):
            if 0 <= step - n < len(stages):
                stages[step - n](n)
    for n in range(chunks):
        take_balance(1, n)
    lam_out[...] = jnp.concatenate([to_row(lam[n]) for n in range(chunks)], axis=1)
    for copy in started:
        copy.wait_send()


def finish(*refs):
    count = len(refs) // 2
    for source, result in zip(refs[:count], refs[count:]):
        result[...] = source[...].reshape(result.shape)


def shards(
    ptdf,
    load,
    ratings,
    line_index,
    gen_bus,
    gen_quad,
    gen_lin,
    gen_max,
    gen_start,
    stor_bus,
    stor_quad,
    stor_rate,
    stor_energy,
    stor_start,
    lam_start,
    mu_start,
    omega_start,
):
    lines_n = lax.axis_size("lines")
    buses_n = lax.axis_size("buses")
    rows, bus_count = load.shape
    line_count = ptdf.shape[0]
    gens = gen_bus.shape[0]
    stors = stor_bus.shape[0]
    units = gens + stors
    share = line_count // buses_n
    chips = buses_n // 2
    piece = units // lines_n
    slots = max(8, (gens + buses_n - 1) // buses_n)
    slots = (slots + 15) // 16 * 16
    chunk = 128 if rows % 128 == 0 else rows
    chunks = rows // chunk
    vmem = pl.BlockSpec(memory_space=pltpu.VMEM)
    hbm = pl.BlockSpec(memory_space=pl.ANY)
    dma = pltpu.SemaphoreType.DMA
    outs = pl.pallas_call(
        functools.partial(kernel, lines_n, buses_n, slots),
        out_shape=(
            jax.ShapeDtypeStruct((rows, gens), F32),
            jax.ShapeDtypeStruct((rows, stors), F32),
            jax.ShapeDtypeStruct((1, rows), F32),
            jax.ShapeDtypeStruct((rows, share), F32),
            jax.ShapeDtypeStruct((rows, stors), F32),
        ),
        in_specs=[vmem] * 15 + [hbm] * 2,
        out_specs=(vmem,) * 5,
        scratch_shapes=[
            pltpu.VMEM((line_count, bus_count), BF16),
            pltpu.VMEM((rows, bus_count), F32),
            pltpu.VMEM((rows, bus_count), BF16),
            pltpu.VMEM((2, chips, share, rows), F32),
            pltpu.VMEM((buses_n, 1, gens), jnp.int32),
            pltpu.VMEM((2, buses_n, slots, line_count // 2), BF16),
            pltpu.VMEM((2, buses_n, slots, line_count // 2), BF16),
            pltpu.VMEM((units, line_count), BF16),
            pltpu.VMEM((2, chips, share, units), BF16),
            pltpu.VMEM((2, chunks, buses_n, share, chunk), BF16),
            pltpu.VMEM((2, chunks, lines_n, piece, chunk), BF16),
            pltpu.VMEM((2, chunks, lines_n, piece, chunk), BF16),
            pltpu.VMEM((2, chunks, lines_n, piece, chunk), BF16),
            pltpu.VMEM((rows, gens), F32),
            pltpu.VMEM((rows, stors), F32),
            pltpu.VMEM((rows, stors), F32),
            pltpu.VMEM((2, chunks, 2, chips, share, chunk), BF16),
            pltpu.VMEM((2, chunks, chips, share, chunk), BF16),
            pltpu.VMEM((2, chunks, chips, share, chunk), BF16),
            pltpu.VMEM((2, chunks, chips, share, chunk), BF16),
            pltpu.VMEM((2, chunks, 1, chunk), F32),
            pltpu.VMEM((2, chunks, buses_n, 1, chunk), F32),
            dma((2,)),
            dma((2, buses_n)),
            dma((2, 2, buses_n)),
            dma((2, chunks, 2, chips)),
            dma((2, chunks, 2, chips)),
            dma((2, chunks, 2, lines_n)),
            dma((2, chunks, 2, lines_n)),
            dma((2, chunks, 2)),
            dma((2, chunks, 2, chips)),
            dma((2, chunks, 2, buses_n)),
        ],
        compiler_params=pltpu.CompilerParams(
            collective_id=0, has_side_effects=True, vmem_limit_bytes=60 * 1024 * 1024
        ),
    )(
        gen_bus[None, :],
        mu_start,
        ratings.reshape(-1, 128),
        line_index.reshape(buses_n, share),
        gen_quad[None, :],
        gen_lin[None, :],
        gen_max[None, :],
        gen_start,
        stor_bus[None, :],
        stor_quad[None, :],
        stor_rate[None, :],
        stor_energy[None, :],
        stor_start,
        lam_start,
        omega_start,
        ptdf,
        load,
    )
    shapes = [x.shape for x in outs]
    shapes[2] = (rows,)
    return pl.pallas_call(
        finish,
        out_shape=tuple(jax.ShapeDtypeStruct(shape, F32) for shape in shapes),
        in_specs=[vmem] * 5,
        out_specs=(vmem,) * 5,
    )(*outs)


def solution(mesh):
    return jax.shard_map(
        shards,
        mesh=mesh,
        in_specs=(
            P("lines", "buses"),
            P(None, "buses"),
            P(),
            P("lines"),
            P("buses"),
            P("buses"),
            P("buses"),
            P("buses"),
            P(None, "buses"),
            P("buses"),
            P("buses"),
            P("buses"),
            P("buses"),
            P(None, "buses"),
            P(),
            P(None, ("lines", "buses")),
            P(None, "buses"),
        ),
        out_specs=(
            P(None, "buses"),
            P(None, "buses"),
            P(),
            P(None, ("lines", "buses")),
            P(None, "buses"),
        ),
        check_vma=False,
    )
```

time: 103 us -> 85.2 us (0.83)
  Pallas kernels: 93.1 us -> 84.4 us
  local copies, waits for them, and re-layouts: 7.86 us -> 0 us
  other arithmetic: 1.26 us -> 0 us
    pallas_call x1, Pallas kernels: 93.1 us -> 82.2 us  [shards(): pl.pallas_call(functools.partial(kernel, lines_n, buses_n, slots), out_sh...]
    unnamed x4 -> x0, local copies, waits for them, and re-layouts: 6.61 us -> none
    pallas_call x0 -> x1, Pallas kernels: none -> 2.2 us  [shards(): pl.pallas_call(finish, out_shape=tuple((jax.ShapeDtypeStruct(shape, F32)...]
    pallas_call x1 -> x0, other arithmetic: 1.26 us -> none  [shards(): pl.pallas_call(functools.partial(kernel, lines_n, buses_n, slots), out_sh...]
    broadcast_in_dim x1 -> x0, local copies, waits for them, and re-layouts: 1.25 us -> none  [shards(): lam_start[None, :]]
where the time goes in v2:
time: 85.2 us; the launch traced here: 85 us
  Pallas kernels  84.4 us (99%)
    pallas_call x1, Pallas kernels, shards(): pl.pallas_call(functools.partial(kernel, lines_n, buses_n, slots), out_sh...  82.2 us
    pallas_call x1, Pallas kernels, shards(): pl.pallas_call(finish, out_shape=tuple((jax.ShapeDtypeStruct(shape, F32)...  2.2 us

profile of v2, /device:TPU:0, one launch (start us, length us, event | category | flops | bytes accessed | tf_op | source)
XLA Modules:
  0.0 85.0 jit_solution(14846989734391483328)
XLA Ops:
  0.6 82.2 %shard_map.200 = (f32[384,256]{1,0:T(8,128)}, f32[384,128]{1,0:T(8,128)}, f32[1,384]{1,0:T(1,128)}, f32[384,128]{1,0:T(8,128)}, f32[384,128]{1,0:T(8,128)}) custom-call(s32[1,256]{1,0:T(1,128)} %bitcast.12, f32[384,128]{1,0:T(8,128)} %mu_in.1, f32[256,128]{1,0:T(8,128)} %bitcast.10, s32[8,128]{1,0:T(8,128)} %bitcast.11, f32[1,256]{1,0:T(1,128)} %bitcast.13, ...), custom_call_target="tpu_custom_call" | custom-call | tf_op jit(solution)/shard_map/pallas_call | solution.py:568
  82.8 2.2 %shard_map.201 = (f32[384,256]{1,0:T(8,128)}, f32[384,128]{1,0:T(8,128)}, f32[384]{0:T(512)}, f32[384,128]{1,0:T(8,128)}, f32[384,128]{1,0:T(8,128)}) custom-call(f32[384,256]{1,0:T(8,128)} %get-tuple-element.10.refs_0_, f32[384,128]{1,0:T(8,128)} %get-tuple-element.11.refs_1_, f32[1,384]{1,0:T(1,128)} %get-tuple-element.12.refs_2_, ...), custom_call_target="tpu_custom_call" | custom-call | tf_op jit(solution)/shard_map/pallas_call | solution.py:637

commit v3 on v2

--- a/solution.py
+++ b/solution.py
@@ -39,7 +39,18 @@
     return iota((n, n), 0) == iota((n, n), 1)
 
 
+def masked_sum(mask, x):
+    high = x.astype(BF16)
+    rest = x - high.astype(F32)
+    mid = rest.astype(BF16)
+    low = (rest - mid.astype(F32)).astype(BF16)
+    mask = mask.astype(BF16)
+    return nn(mask, high) + (nn(mask, mid) + nn(mask, low))
+
+
 def flipped(x):
+    if x.shape[0] % 128 == 0 and x.shape[1] % 128 == 0:
+        return x.T
     return nt(eye(x.shape[1]).astype(F32), x, HIGHEST)
 
 
@@ -69,20 +80,20 @@
     buses_n,
     slots,
     gen_bus,
-    mu_in,
-    ratings,
+    mu_in_hbm,
+    ratings_hbm,
     line_index,
     gen_quad,
     gen_lin,
     gen_max,
-    gen_start,
+    gen_start_hbm,
     stor_bus,
     stor_quad,
     stor_rate,
     stor_energy,
-    stor_start,
+    stor_start_hbm,
     lam_in,
-    omega_in,
+    omega_in_hbm,
     ptdf_hbm,
     load_hbm,
     gen_out,
@@ -112,6 +123,11 @@
     line_recv,
     bal_send,
     bal_recv,
+    gen_start,
+    stor_start,
+    omega_in,
+    mu_in,
+    ratings,
     in_sem,
     idx_sem,
     a_sem,
@@ -146,8 +162,22 @@
 
     load_copy = pltpu.make_async_copy(load_hbm, load, in_sem.at[0])
     ptdf_copy = pltpu.make_async_copy(ptdf_hbm, ptdf, in_sem.at[1])
+    small_copies = [
+        pltpu.make_async_copy(source, into, in_sem.at[2 + n])
+        for n, (source, into) in enumerate(
+            (
+                (mu_in_hbm, mu_in),
+                (ratings_hbm, ratings),
+                (gen_start_hbm, gen_start),
+                (stor_start_hbm, stor_start),
+                (omega_in_hbm, omega_in),
+            )
+        )
+    ]
+    for copy in small_copies:
+        copy.start()
+    ptdf_copy.start()
     load_copy.start()
-    ptdf_copy.start()
 
     barrier = pltpu.get_barrier_semaphore()
     for off in range(1, buses_n):
@@ -160,6 +190,7 @@
         )
 
     gen_all[j] = gen_bus[...]
+    small_copies[0].wait()
     mu = flipped(mu_in[...])
     for n in range(chunks):
         dual_all[0, n, j] = mu[:, cut(n)].astype(BF16)
@@ -216,6 +247,57 @@
 
     gather = [gather_start(0, n) for n in range(chunks)]
 
+    for copy in idx_copies:
+        copy.wait_recv()
+    ids = jnp.concatenate([gen_all[a] for a in range(buses_n)], axis=0)
+    ids = ids.astype(F32).T.astype(jnp.int32)
+    local = ids - j * bus_count
+    hit = (local >= 0) & (local < bus_count)
+    upto = (iota((gens, gens), 1) <= iota((gens, gens), 0)).astype(BF16)
+    rank = nn(upto, hit.astype(BF16)) - 1.0
+    rank = jnp.where(hit, rank, 512.0)
+    local = jnp.where(hit, local, 0)
+    spread = (iota((buses_n, width), 1) // slots == iota((buses_n, width), 0)).astype(BF16)
+    rank_wide = nn(rank.astype(BF16), spread)
+    high_wide = nn((local // 128).astype(BF16), spread)
+    low_wide = nn((local % 128).astype(BF16), spread)
+    taken = rank_wide == (iota((gens, width), 1) % slots).astype(F32)
+    slot_bus = jnp.sum(jnp.where(taken, high_wide * 128.0 + low_wide + 1.0, 0.0), axis=0, keepdims=True)
+    slot_bus = to_column(slot_bus).astype(jnp.int32) - 1
+    slot_hit = (iota((width, bus_count), 1) == slot_bus).astype(BF16)
+    ptdf_copy.wait()
+    tile = 256 if line_count % 512 == 0 else 128
+    half = line_count // 2
+    a_copies = [[], []]
+    for h in range(2):
+
+        def columns_step(t, carry):
+            at = pl.multiple_of(t * tile, tile)
+            block = ptdf[pl.ds(pl.multiple_of(h * half + t * tile, tile), tile), :]
+            value = nt(slot_hit, block).astype(BF16)
+            a_send[h, :, :, pl.ds(at, tile)] = value.reshape(buses_n, slots, tile)
+            return carry
+
+        lax.fori_loop(0, half // tile, columns_step, 0)
+        for off in range(1, buses_n):
+            to = lax.rem(j + off, buses_n)
+            a_copies[h].append(
+                go(
+                    remote(
+                        a_send.at[h, to],
+                        a_recv.at[h, j],
+                        a_sem.at[h, 0, off],
+                        a_sem.at[h, 1, off],
+                        (i, to),
+                    )
+                )
+            )
+        a_recv[h, j] = a_send[h, j]
+
+    stor_column = to_column(stor_bus[...].astype(F32)).astype(jnp.int32)
+    stor_hit = (iota((stors, bus_count), 1) == stor_column).astype(BF16)
+    for copy in small_copies[1:]:
+        copy.wait()
     load_copy.wait()
     load_value = load[...]
     load_total = jnp.sum(load_value, axis=1, keepdims=True)
@@ -230,7 +312,7 @@
     wanted = to_column(wanted).astype(jnp.int32)
     lanes = ratings.shape[1]
     high_hit = (iota((share, ratings.shape[0]), 1) == wanted // lanes).astype(F32)
-    rated = nn(high_hit, ratings[...], HIGHEST)
+    rated = masked_sum(high_hit, ratings[...])
     limit = jnp.sum(
         jnp.where(iota((share, lanes), 1) == wanted % lanes, rated, 0.0), axis=1, keepdims=True
     )
@@ -242,56 +324,7 @@
     later = jnp.where(same & (col_id >= row_id), 1.0, 0.0)
     earlier = jnp.where(same & (col_id <= row_id), 1.0, 0.0)
 
-    for copy in idx_copies:
-        copy.wait_recv()
-    ids = jnp.concatenate([gen_all[a] for a in range(buses_n)], axis=0)
-    ids = flipped(ids.astype(F32)).astype(jnp.int32)
-    local = ids - j * bus_count
-    hit = (local >= 0) & (local < bus_count)
-    upto = (iota((gens, gens), 1) <= iota((gens, gens), 0)).astype(BF16)
-    rank = nn(upto, hit.astype(BF16)) - 1.0
-    rank = jnp.where(hit, rank, 512.0)
-    local = jnp.where(hit, local, 0)
-    spread = (iota((buses_n, width), 1) // slots == iota((buses_n, width), 0)).astype(BF16)
-    rank_wide = nn(rank.astype(BF16), spread)
-    high_wide = nn((local // 128).astype(BF16), spread)
-    low_wide = nn((local % 128).astype(BF16), spread)
-    taken = rank_wide == (iota((gens, width), 1) % slots).astype(F32)
-    slot_bus = jnp.sum(jnp.where(taken, high_wide * 128.0 + low_wide + 1.0, 0.0), axis=0, keepdims=True)
-    slot_bus = to_column(slot_bus).astype(jnp.int32) - 1
-    slot_hit = (iota((width, bus_count), 1) == slot_bus).astype(BF16)
-    stor_column = to_column(stor_bus[...].astype(F32)).astype(jnp.int32)
-    stor_hit = (iota((stors, bus_count), 1) == stor_column).astype(BF16)
-    ptdf_copy.wait()
-    tile = 128
-    half = line_count // 2
-    a_copies = [[], []]
-    for h in range(2):
-
-        def columns_step(t, carry):
-            at = pl.multiple_of(t * tile, tile)
-            block = ptdf[pl.ds(pl.multiple_of(h * half + t * tile, tile), tile), :]
-            value = nt(slot_hit, block).astype(BF16)
-            a_send[h, :, :, pl.ds(at, tile)] = value.reshape(buses_n, slots, tile)
-            return carry
-
-        lax.fori_loop(0, half // tile, columns_step, 0)
-        for off in range(1, buses_n):
-            to = lax.rem(j + off, buses_n)
-            a_copies[h].append(
-                go(
-                    remote(
-                        a_send.at[h, to],
-                        a_recv.at[h, j],
-                        a_sem.at[h, 0, off],
-                        a_sem.at[h, 1, off],
-                        (i, to),
-                    )
-                )
-            )
-        a_recv[h, j] = a_send[h, j]
-
-    wide = max(tile, 2 * share)
+    wide = max(128, 2 * share)
     group = wide // (2 * share)
 
     def load_step(t, carry):
@@ -313,7 +346,7 @@
     own_rank = nn(upto, target_hit.astype(BF16))
     own_rank = jnp.sum(jnp.where(target_hit, own_rank, 0.0), axis=1, keepdims=True).astype(jnp.int32) - 1
     place = (iota((gens, width), 1) == target * slots + own_rank).astype(BF16)
-    back = nn(later, omega_in[...], HIGHEST)
+    back = masked_sum(later, omega_in[...])
 
     gather = [gather_forward(0, n, gather[n]) for n in range(chunks)]
     for h in range(2):
@@ -342,18 +375,15 @@
         for copy in gather[n]:
             copy.wait_recv()
         duals = dual_all[k, n].reshape(line_count, chunk)
+        value = nn(a_t[...], duals).reshape(lines_n, piece, chunk)
+        price_part[k, n] = value.astype(BF16)
         copies = []
-        for off in range(1, lines_n + 1):
+        for off in range(1, lines_n):
             to = lax.rem(i + off, lines_n)
-            at = pl.multiple_of(to * piece, piece)
-            value = nn(a_t[pl.ds(at, piece), :], duals)
-            if off == lines_n:
-                break
-            price_part[k, n, off] = value.astype(BF16)
             copies.append(
                 go(
                     remote(
-                        price_part.at[k, n, off],
+                        price_part.at[k, n, to],
                         price_recv.at[k, n, off],
                         pr_sem.at[k, n, 0, off],
                         pr_sem.at[k, n, 1, off],
@@ -361,10 +391,11 @@
                     )
                 )
             )
-        pending[n] = (value, copies)
+        pending[n] = copies
 
     def share_stage(k, n):
-        total, copies = pending[n]
+        copies = pending[n]
+        total = price_part[k, n, i].astype(F32)
         for off in range(1, lines_n):
             copies[off - 1].wait_recv()
             total = total + price_recv[k, n, off].astype(F32)
@@ -480,12 +511,12 @@
             )
         pending[n] = copies
         if n == chunks - 1:
-            charge = nn(earlier, bar_keep[...], HIGHEST)
+            charge = masked_sum(earlier, bar_keep[...])
             shifted = hold["omega"] + SIGMA_STORE * charge
             omega = shifted - SIGMA_STORE * jnp.clip(shifted / SIGMA_STORE, -high_bound, high_bound)
             if k == 0:
                 hold["omega"] = omega
-                hold["back"] = nn(later, omega, HIGHEST)
+                hold["back"] = masked_sum(later, omega)
             else:
                 omega_out[...] = omega
 
@@ -574,7 +605,7 @@
             jax.ShapeDtypeStruct((rows, share), F32),
             jax.ShapeDtypeStruct((rows, stors), F32),
         ),
-        in_specs=[vmem] * 15 + [hbm] * 2,
+        in_specs=[hbm if n in (1, 2, 7, 12, 14, 15, 16) else vmem for n in range(17)],
         out_specs=(vmem,) * 5,
         scratch_shapes=[
             pltpu.VMEM((line_count, bus_count), BF16),
@@ -599,7 +630,12 @@
             pltpu.VMEM((2, chunks, chips, share, chunk), BF16),
             pltpu.VMEM((2, chunks, 1, chunk), F32),
             pltpu.VMEM((2, chunks, buses_n, 1, chunk), F32),
-            dma((2,)),
+            pltpu.VMEM((rows, gens), F32),
+            pltpu.VMEM((rows, stors), F32),
+            pltpu.VMEM((rows, stors), F32),
+            pltpu.VMEM((rows, share), F32),
+            pltpu.VMEM((ratings.shape[0] // 128, 128), F32),
+            dma((7,)),
             dma((2, buses_n)),
             dma((2, 2, buses_n)),
             dma((2, chunks, 2, chips)),

time: 85.2 us -> 84.9 us (level)
  no operation moved by 1% of the time
where the time goes in v3:
time: 84.9 us; the launch traced here: 84.7 us
  Pallas kernels  84.1 us (99%)
    pallas_call x1, Pallas kernels, shards(): pl.pallas_call(functools.partial(kernel, lines_n, buses_n, slots), out_sh...  81.9 us
    pallas_call x1, Pallas kernels, shards(): pl.pallas_call(finish, out_shape=tuple((jax.ShapeDtypeStruct(shape, F32)...  2.2 us

profile of v3, /device:TPU:0, one launch (start us, length us, event | category | flops | bytes accessed | tf_op | source)
XLA Modules:
  0.0 84.7 jit_solution(6460217334778764975)
XLA Ops:
  0.6 81.9 %shard_map.200 = (f32[384,256]{1,0:T(8,128)}, f32[384,128]{1,0:T(8,128)}, f32[1,384]{1,0:T(1,128)}, f32[384,128]{1,0:T(8,128)}, f32[384,128]{1,0:T(8,128)}) custom-call(s32[1,256]{1,0:T(1,128)} %bitcast.12, f32[384,128]{1,0:T(8,128)} %mu_in_hbm.1, f32[256,128]{1,0:T(8,128)} %bitcast.10, s32[8,128]{1,0:T(8,128)} %bitcast.11, f32[1,256]{1,0:T(1,128)} %bitcast.13, ...), custom_call_target="tpu_custom_call" | custom-call | tf_op jit(solution)/shard_map/pallas_call | solution.py:599
  82.5 2.2 %shard_map.201 = (f32[384,256]{1,0:T(8,128)}, f32[384,128]{1,0:T(8,128)}, f32[384]{0:T(512)}, f32[384,128]{1,0:T(8,128)}, f32[384,128]{1,0:T(8,128)}) custom-call(f32[384,256]{1,0:T(8,128)} %get-tuple-element.10.refs_0_, f32[384,128]{1,0:T(8,128)} %get-tuple-element.11.refs_1_, f32[1,384]{1,0:T(1,128)} %get-tuple-element.12.refs_2_, ...), custom_call_target="tpu_custom_call" | custom-call | tf_op jit(solution)/shard_map/pallas_call | solution.py:673
